TPU v7x, 32 devices: a whole 2x2x4 slice. The times are simulated.
32 devices in a mesh: fsdp: 8 (over z, y), tp: 4 (over x, core).
Axes of the slice: x: 2, y: 2, z: 4, core: 2. Of those that a mesh axis runs over, the one named last changes fastest.
Arguments:
- inputs: bfloat16 [16, 736, 1152], P('fsdp', 'tp'), may hold values from -6 to 6
- cotangent: bfloat16 [16, 736, 1152], P('fsdp', 'tp'), may hold values from -6 to 6
- lengths: int32 [16], P('fsdp'), may hold values from 1 to 729, as said below
- ln1_gain: bfloat16 [1152], P('fsdp'), may hold values from 0.099609375 to 1.8984375
- ln1_bias: bfloat16 [1152], P('fsdp'), may hold values from -0.3125 to 0.3125
- q_weight: bfloat16 [1152, 1152], P('fsdp', 'tp'), may hold values from -0.1875 to 0.1875
- q_bias: bfloat16 [1152], P('tp'), may hold values from -3 to 3
- k_weight: bfloat16 [1152, 1152], P('fsdp', 'tp'), may hold values from -0.1875 to 0.1875
- v_weight: bfloat16 [1152, 1152], P('fsdp', 'tp'), may hold values from -0.1875 to 0.1875
- v_bias: bfloat16 [1152], P('tp'), may hold values from -0.1875 to 0.1875
- out_weight: bfloat16 [1152, 1152], P('tp', 'fsdp'), may hold values from -2.5 to 2.5
- out_bias: bfloat16 [1152], P('fsdp'), may hold values from -1.75 to 1.75
- ln2_gain: bfloat16 [1152], P('fsdp'), may hold values from 0.099609375 to 1.8984375
- ln2_bias: bfloat16 [1152], P('fsdp'), may hold values from -1.75 to 1.75
- up_weight: bfloat16 [1152, 4304], P('fsdp', 'tp'), may hold values from -0.1875 to 0.1875
- up_bias: bfloat16 [4304], P('tp'), may hold values from -1.75 to 1.75
- down_weight: bfloat16 [4304, 1152], P('tp', 'fsdp'), may hold values from -0.09375 to 0.09375
- down_bias: bfloat16 [1152], P('fsdp'), may hold values from -1.75 to 1.75
Outputs:
- layer_out: bfloat16 [16, 736, 1152], P('fsdp', 'tp')
- input_grad: float32 [16, 736, 1152], P('fsdp', 'tp')
- ln1_gain_grad: float32 [1152], P('fsdp')
- ln1_bias_grad: float32 [1152], P('fsdp')
- q_weight_grad: float32 [1152, 1152], P('fsdp', 'tp')
- q_bias_grad: float32 [1152], P('tp')
- k_weight_grad: float32 [1152, 1152], P('fsdp', 'tp')
- v_weight_grad: float32 [1152, 1152], P('fsdp', 'tp')
- v_bias_grad: float32 [1152], P('tp')
- out_weight_grad: float32 [1152, 1152], P('tp', 'fsdp')
- out_bias_grad: float32 [1152], P('fsdp')
- ln2_gain_grad: float32 [1152], P('fsdp')
- ln2_bias_grad: float32 [1152], P('fsdp')
- up_weight_grad: float32 [1152, 4304], P('fsdp', 'tp')
- up_bias_grad: float32 [4304], P('tp')
- down_weight_grad: float32 [4304, 1152], P('tp', 'fsdp')
- down_bias_grad: float32 [1152], P('fsdp')
Inputs may be any that keep to these rules, and one draw needn't show every extreme that they name: `lengths`: each slot either holds one image of 729 tokens or is empty with length 1; exactly 11 slots hold images, which ones drawn from the seed.
All inputs are finite; a program needn't handle non-finite values.
Results may differ from a plain program's by a relative error of at most 0.013.
Values may be sent and summed in bfloat16 or wider, within the bound.
No kernel may reach another device: no remote copies, remote signals or barrier semaphores. Data moves between devices by JAX's collectives and lax.ppermute only.
A program may use at most 192 MiB of HBM per device.

v0:
```python
import jax
import jax.numpy as jnp
from jax import lax
from jax.sharding import PartitionSpec as P

HD = 72
epsilon = 1e-06
negative_big = -1e30


def layer_norm(row_block, gain_vec, shift_vec):
    average = jnp.mean(row_block, -1, keepdims=True)
    center = row_block - average
    variance = jnp.mean(center * center, -1, keepdims=True)
    return center * lax.rsqrt(variance + epsilon) * gain_vec + shift_vec


def gelu_tanh(values_in):
    return jax.nn.gelu(values_in, approximate=True)


def plain_dot(left, right):
    return jnp.dot(left, right, preferred_element_type=jnp.float32)


def contract_rows(left, right):
    return lax.dot_general(
        left, right, (((0,), (0,)), ((), ())), preferred_element_type=jnp.float32
    )


def contract_cols(left, right):
    return lax.dot_general(
        left, right, (((1,), (1,)), ((), ())), preferred_element_type=jnp.float32
    )


def local(
    inputs,
    cotangent,
    lengths,
    ln1_gain,
    ln1_bias,
    q_weight,
    q_bias,
    k_weight,
    v_weight,
    v_bias,
    out_weight,
    out_bias,
    ln2_gain,
    ln2_bias,
    up_weight,
    up_bias,
    down_weight,
    down_bias,
):
    tp_count = lax.axis_size("tp")
    tp_index = lax.axis_index("tp")
    fsdp_index = lax.axis_index("fsdp")
    micro_count = inputs.shape[0]
    local_rows = inputs.shape[1]
    model_width = inputs.shape[2]
    seq_len = local_rows * tp_count
    head_width = q_weight.shape[1]
    heads_here = head_width // HD
    unit_width = up_weight.shape[1]
    scale_value = HD ** (-0.5)
    q_shift = q_bias.astype(jnp.float32)
    v_shift = v_bias.astype(jnp.float32)
    up_shift = up_bias.astype(jnp.float32)

    def fetch_weights():
        attn_full = (
            lax.all_gather(ln1_gain, "fsdp", axis=0, tiled=True),
            lax.all_gather(ln1_bias, "fsdp", axis=0, tiled=True),
            lax.all_gather(q_weight, "fsdp", axis=0, tiled=True),
            lax.all_gather(k_weight, "fsdp", axis=0, tiled=True),
            lax.all_gather(v_weight, "fsdp", axis=0, tiled=True),
            lax.all_gather(out_weight, "fsdp", axis=1, tiled=True),
            lax.all_gather(out_bias, "fsdp", axis=0, tiled=True),
        )
        mlp_full = (
            lax.all_gather(ln2_gain, "fsdp", axis=0, tiled=True),
            lax.all_gather(ln2_bias, "fsdp", axis=0, tiled=True),
            lax.all_gather(up_weight, "fsdp", axis=0, tiled=True),
            lax.all_gather(down_weight, "fsdp", axis=1, tiled=True),
            lax.all_gather(down_bias, "fsdp", axis=0, tiled=True),
        )
        return (attn_full, mlp_full)

    def masked_scores(queries, keys_all, key_valid):
        query_heads = queries.reshape(seq_len, heads_here, HD)
        key_heads = keys_all.reshape(seq_len, heads_here, HD)
        scores = (
            jnp.einsum("qhd,khd->hqk", query_heads, key_heads, preferred_element_type=jnp.float32)
            * scale_value
        )
        return jnp.where(key_valid[None, None, :], scores, negative_big)

    def forward(slot_rows, length, attn_full, mlp_full):
        gain_one, shift_one, wq_full, wk_full, wv_full, wo_full, bo_full = attn_full
        gain_two, shift_two, w_up, w_down, bd_full = mlp_full
        key_valid = jnp.arange(seq_len, dtype=jnp.int32) < length
        norm_one = layer_norm(
            slot_rows, gain_one.astype(jnp.float32), shift_one.astype(jnp.float32)
        ).astype(jnp.bfloat16)
        norm_full = lax.all_gather(norm_one, "tp", axis=0, tiled=True)
        queries = (plain_dot(norm_full, wq_full) + q_shift).astype(jnp.bfloat16)
        keys_all = plain_dot(norm_full, wk_full).astype(jnp.bfloat16)
        values_all = (plain_dot(norm_full, wv_full) + v_shift).astype(jnp.bfloat16)
        scores = masked_scores(queries, keys_all, key_valid)
        row_max = jnp.max(scores, -1, keepdims=True)
        row_total = jnp.sum(jnp.exp(scores - row_max), -1, keepdims=True)
        log_total = row_max + jnp.log(row_total)
        soft_low = jnp.exp(scores - log_total).astype(jnp.bfloat16)
        value_heads = values_all.reshape(seq_len, heads_here, HD)
        mixed_heads = jnp.einsum(
            "hqk,khd->qhd", soft_low, value_heads, preferred_element_type=jnp.float32
        )
        mixed_heads = mixed_heads.astype(jnp.bfloat16).reshape(seq_len, head_width)
        attended = lax.psum_scatter(
            plain_dot(mixed_heads, wo_full), "tp", scatter_dimension=0, tiled=True
        )
        middle = slot_rows + attended + bo_full.astype(jnp.float32)
        norm_two = layer_norm(
            middle, gain_two.astype(jnp.float32), shift_two.astype(jnp.float32)
        ).astype(jnp.bfloat16)
        norm_two_full = lax.all_gather(norm_two, "tp", axis=0, tiled=True)
        hidden = plain_dot(norm_two_full, w_up) + up_shift
        active = gelu_tanh(hidden).astype(jnp.bfloat16)
        mlp_rows = lax.psum_scatter(
            plain_dot(active, w_down), "tp", scatter_dimension=0, tiled=True
        )
        out_rows = middle + mlp_rows + bd_full.astype(jnp.float32)
        kept_state = (
            norm_full,
            queries,
            keys_all,
            values_all,
            log_total,
            mixed_heads,
            middle,
            norm_two_full,
            hidden,
            active,
        )
        return (out_rows, kept_state)

    outputs = []
    for slot_index in range(micro_count):
        attn_full, mlp_full = fetch_weights()
        out_rows, kept_state = forward(
            inputs[slot_index].astype(jnp.float32), lengths[slot_index], attn_full, mlp_full
        )
        outputs.append(out_rows.astype(jnp.bfloat16))
    grad_list = []
    totals = None
    for slot_index in range(micro_count):
        attn_full, mlp_full = fetch_weights()
        slot_rows = inputs[slot_index].astype(jnp.float32)
        kept_state = forward(slot_rows, lengths[slot_index], attn_full, mlp_full)[1]
        backward_length = lengths[slot_index]
        (
            backward_gain_one,
            backward_shift_one,
            backward_wq_full,
            backward_wk_full,
            backward_wv_full,
            backward_wo_full,
            backward_bo_full,
        ) = attn_full
        backward_gain_two, backward_shift_two, backward_w_up, backward_w_down, backward_bd_full = (
            mlp_full
        )
        (
            backward_norm_full,
            backward_queries,
            backward_keys_all,
            backward_values_all,
            backward_log_total,
            backward_mixed_heads,
            backward_middle,
            backward_norm_two_full,
            backward_hidden,
            backward_active,
        ) = kept_state
        backward_key_valid = jnp.arange(seq_len, dtype=jnp.int32) < backward_length
        row_valid = (
            jnp.arange(local_rows, dtype=jnp.int32) + tp_index * local_rows < backward_length
        ).astype(jnp.float32)
        grad_out = cotangent[slot_index].astype(jnp.float32) * row_valid[:, None]
        backward_down_sum = jnp.sum(grad_out, 0)
        grad_out_full = lax.all_gather(grad_out.astype(jnp.bfloat16), "tp", axis=0, tiled=True)
        backward_grad_w_down = contract_rows(backward_active, grad_out_full)
        grad_active = contract_cols(grad_out_full, backward_w_down)
        gelu_pull = jax.vjp(gelu_tanh, backward_hidden)[1]
        grad_hidden = gelu_pull(grad_active)[0].astype(jnp.bfloat16)
        backward_up_sum = jnp.sum(grad_hidden.astype(jnp.float32), 0)
        backward_grad_w_up = contract_rows(backward_norm_two_full, grad_hidden)
        grad_norm_two = lax.psum_scatter(
            contract_cols(grad_hidden, backward_w_up), "tp", scatter_dimension=0, tiled=True
        )
        norm_two_pull = jax.vjp(
            layer_norm,
            backward_middle,
            backward_gain_two.astype(jnp.float32),
            backward_shift_two.astype(jnp.float32),
        )[1]
        middle_part, backward_gain_two_grad, backward_shift_two_grad = norm_two_pull(grad_norm_two)
        grad_middle = grad_out + middle_part
        backward_out_sum = jnp.sum(grad_middle, 0)
        grad_middle_full = lax.all_gather(
            grad_middle.astype(jnp.bfloat16), "tp", axis=0, tiled=True
        )
        backward_grad_w_out = contract_rows(backward_mixed_heads, grad_middle_full)
        grad_mixed = (
            contract_cols(grad_middle_full, backward_wo_full)
            .astype(jnp.bfloat16)
            .reshape(seq_len, heads_here, HD)
        )
        soft_weights = jnp.exp(
            masked_scores(backward_queries, backward_keys_all, backward_key_valid)
            - backward_log_total
        )
        backward_soft_low = soft_weights.astype(jnp.bfloat16)
        backward_query_heads = backward_queries.reshape(seq_len, heads_here, HD)
        backward_key_heads = backward_keys_all.reshape(seq_len, heads_here, HD)
        backward_value_heads = backward_values_all.reshape(seq_len, heads_here, HD)
        grad_soft = jnp.einsum(
            "qhd,khd->hqk", grad_mixed, backward_value_heads, preferred_element_type=jnp.float32
        )
        row_inner = jnp.sum(soft_weights * grad_soft, -1, keepdims=True)
        grad_scores = (soft_weights * (grad_soft - row_inner)).astype(jnp.bfloat16)
        grad_queries = (
            (
                jnp.einsum(
                    "hqk,khd->qhd",
                    grad_scores,
                    backward_key_heads,
                    preferred_element_type=jnp.float32,
                )
                * scale_value
            )
            .astype(jnp.bfloat16)
            .reshape(seq_len, head_width)
        )
        grad_keys = (
            (
                jnp.einsum(
                    "hqk,qhd->khd",
                    grad_scores,
                    backward_query_heads,
                    preferred_element_type=jnp.float32,
                )
                * scale_value
            )
            .astype(jnp.bfloat16)
            .reshape(seq_len, head_width)
        )
        grad_values = (
            jnp.einsum(
                "hqk,qhd->khd", backward_soft_low, grad_mixed, preferred_element_type=jnp.float32
            )
            .astype(jnp.bfloat16)
            .reshape(seq_len, head_width)
        )
        backward_query_sum = jnp.sum(grad_queries.astype(jnp.float32), 0)
        backward_value_sum = jnp.sum(grad_values.astype(jnp.float32), 0)
        backward_grad_wq = contract_rows(backward_norm_full, grad_queries)
        backward_grad_wk = contract_rows(backward_norm_full, grad_keys)
        backward_grad_wv = contract_rows(backward_norm_full, grad_values)
        part_q = contract_cols(grad_queries, backward_wq_full)
        part_k = contract_cols(grad_keys, backward_wk_full)
        part_v = contract_cols(grad_values, backward_wv_full)
        grad_norm_one = lax.psum_scatter(
            part_q + part_k + part_v, "tp", scatter_dimension=0, tiled=True
        )
        norm_one_pull = jax.vjp(
            layer_norm,
            slot_rows,
            backward_gain_one.astype(jnp.float32),
            backward_shift_one.astype(jnp.float32),
        )[1]
        rows_part, backward_gain_one_grad, backward_shift_one_grad = norm_one_pull(grad_norm_one)
        grad_rows = grad_middle + rows_part
        slot_grads = (
            backward_gain_one_grad,
            backward_shift_one_grad,
            backward_grad_wq,
            backward_query_sum,
            backward_grad_wk,
            backward_grad_wv,
            backward_value_sum,
            backward_grad_w_out,
            backward_out_sum,
            backward_gain_two_grad,
            backward_shift_two_grad,
            backward_grad_w_up,
            backward_up_sum,
            backward_grad_w_down,
            backward_down_sum,
        )
        grad_rows, slot_grads = (grad_rows, slot_grads)
        grad_list.append(grad_rows)
        if totals is None:
            totals = slot_grads
        else:
            totals = jax.tree.map(jnp.add, totals, slot_grads)
    (
        gain_one_grad,
        shift_one_grad,
        grad_wq,
        query_sum,
        grad_wk,
        grad_wv,
        value_sum,
        grad_w_out,
        out_sum,
        gain_two_grad,
        shift_two_grad,
        grad_w_up,
        up_sum,
        grad_w_down,
        down_sum,
    ) = totals
    summed_weights = (
        lax.psum_scatter(grad_wq, "fsdp", scatter_dimension=0, tiled=True),
        lax.psum_scatter(grad_wk, "fsdp", scatter_dimension=0, tiled=True),
        lax.psum_scatter(grad_wv, "fsdp", scatter_dimension=0, tiled=True),
        lax.psum_scatter(grad_w_out, "fsdp", scatter_dimension=1, tiled=True),
        lax.psum_scatter(grad_w_up, "fsdp", scatter_dimension=0, tiled=True),
        lax.psum_scatter(grad_w_down, "fsdp", scatter_dimension=1, tiled=True),
    )
    width_stack = jnp.stack(
        [gain_one_grad, shift_one_grad, out_sum, gain_two_grad, shift_two_grad, down_sum], 0
    )
    head_stack = jnp.zeros((2, head_width * tp_count), jnp.float32)
    head_stack = lax.dynamic_update_slice_in_dim(
        head_stack, jnp.stack([query_sum, value_sum], 0), tp_index * head_width, 1
    )
    unit_line = jnp.zeros((unit_width * tp_count,), jnp.float32)
    unit_line = lax.dynamic_update_slice_in_dim(unit_line, up_sum, tp_index * unit_width, 0)
    summed_small = lax.psum((width_stack, head_stack, unit_line), ("fsdp", "tp"))
    shard_size = model_width // lax.axis_size("fsdp")
    width_pieces = lax.dynamic_slice_in_dim(summed_small[0], fsdp_index * shard_size, shard_size, 1)
    head_pieces = lax.dynamic_slice_in_dim(summed_small[1], tp_index * head_width, head_width, 1)
    unit_piece = lax.dynamic_slice_in_dim(summed_small[2], tp_index * unit_width, unit_width, 0)
    return (
        jnp.stack(outputs, 0),
        jnp.stack(grad_list, 0),
        width_pieces[0],
        width_pieces[1],
        summed_weights[0],
        head_pieces[0],
        summed_weights[1],
        summed_weights[2],
        head_pieces[1],
        summed_weights[3],
        width_pieces[2],
        width_pieces[3],
        width_pieces[4],
        summed_weights[4],
        unit_piece,
        summed_weights[5],
        width_pieces[5],
    )


def solution(mesh):
    in_specs = (
        P("fsdp", "tp", None),
        P("fsdp", "tp", None),
        P("fsdp"),
        P("fsdp"),
        P("fsdp"),
        P("fsdp", "tp"),
        P("tp"),
        P("fsdp", "tp"),
        P("fsdp", "tp"),
        P("tp"),
        P("tp", "fsdp"),
        P("fsdp"),
        P("fsdp"),
        P("fsdp"),
        P("fsdp", "tp"),
        P("tp"),
        P("tp", "fsdp"),
        P("fsdp"),
    )
    out_specs = (
        P("fsdp", "tp", None),
        P("fsdp", "tp", None),
        P("fsdp"),
        P("fsdp"),
        P("fsdp", "tp"),
        P("tp"),
        P("fsdp", "tp"),
        P("fsdp", "tp"),
        P("tp"),
        P("tp", "fsdp"),
        P("fsdp"),
        P("fsdp"),
        P("fsdp"),
        P("fsdp", "tp"),
        P("tp"),
        P("tp", "fsdp"),
        P("fsdp"),
    )
    return jax.shard_map(local, mesh=mesh, in_specs=in_specs, out_specs=out_specs, check_vma=False)
```

profile of v0, /device:TPU:0, one launch (start us, length us, event | category | flops | bytes accessed | tf_op | source)
XLA Modules:
  0.0 1294.0 jit_solution(5558494795576318744)
XLA Ops:
  14.4 38.8 %all-reduce.15 = (bf16[1152]{0:T(1024)(128)(2,1)S(1)}, bf16[1152]{0:T(1024)(128)(2,1)S(1)}, bf16[1152]{0:T(1024)(128)(2,1)S(1)}, bf16[1152]{0:T(1024)(128)(2,1)S...) all-reduce(bf16[1152]{0:T(1024)(128)(2,1)S(1)} %dynamic-update-slic, ...), channel_id=1, replica_groups=mesh['fsdp'=8,'tp'=4] {'fsdp'}, use_global_device_ids=true, to_apply=%add.1 | all-reduce | flops 6912 | bytes 27648
  60.0 32.5 %all_gather.44 = bf16[1152,288]{1,0:T(8,128)(2,1)S(1)} all-gather(bf16[144,288]{1,0:T(8,128)(2,1)S(1)} %copy-done.54), channel_id=1, replica_groups=mesh['fsdp'=8,'tp'=4] {'fsdp'}, dimensions={0}, use_global_device_ids=true | all-gather | bytes 746496 | tf_op jit(solution)/shard_map/all_gather | solution.py:77
  92.5 32.2 %all_gather.45 = bf16[1152,288]{1,0:T(8,128)(2,1)S(1)} all-gather(bf16[144,288]{1,0:T(8,128)(2,1)S(1)} %copy-done.55), channel_id=1, replica_groups=mesh['fsdp'=8,'tp'=4] {'fsdp'}, dimensions={0}, use_global_device_ids=true | all-gather | bytes 746496 | tf_op jit(solution)/shard_map/all_gather | solution.py:78
  126.1 34.5 %all_gather.43 = bf16[1152,288]{1,0:T(8,128)(2,1)} all-gather(bf16[144,288]{1,0:T(8,128)(2,1)S(1)} %copy-done.56), channel_id=1, replica_groups=mesh['fsdp'=8,'tp'=4] {'fsdp'}, dimensions={0}, use_global_device_ids=true | all-gather | bytes 746496 | tf_op jit(solution)/shard_map/all_gather | solution.py:79
  160.6 32.0 %all_gather.46 = bf16[288,1152]{0,1:T(8,128)(2,1)S(1)} all-gather(bf16[288,144]{0,1:T(8,128)(2,1)S(1)} %copy-done.57), channel_id=1, replica_groups=mesh['fsdp'=8,'tp'=4] {'fsdp'}, dimensions={1}, use_global_device_ids=true | all-gather | bytes 746496 | tf_op jit(solution)/shard_map/all_gather | solution.py:80
  231.9 15.0 %reduce-scatter.47.cloned.1.call-done = f32[184,1152]{1,0:T(8,128)} async-done(((f32[736,1152]{1,0:T(8,128)}), f32[184,1152]{1,0:T(8,128)}) %reduce-scatter.47.cloned.1.call-update) | async-done | bytes 847888
  247.0 42.0 %reduce-scatter.43.cloned.1.call-done = f32[184,1152]{1,0:T(8,128)} async-done(((f32[736,1152]{1,0:T(8,128)}), f32[184,1152]{1,0:T(8,128)}) %reduce-scatter.43.cloned.1.call-update) | async-done | bytes 847888
  294.4 17.0 %all-gather.23.cloned.1.call-done = bf16[736,1152]{1,0:T(8,128)(2,1)} async-done(((bf16[184,1152]{1,0:T(8,128)(2,1)}), bf16[736,1152]{1,0:T(8,128)(2,1)}) %all-gather.23.cloned.1.call-update) | async-done | bytes 1695760 | tf_op jit(solution)/shard_map/all_gather | solution.py:194
  311.4 57.1 %all-gather.17.cloned.1.call-done = bf16[1076,1152]{0,1:T(8,128)(2,1)} async-done(((bf16[1076,144]{0,1:T(8,128)(2,1)}), bf16[1076,1152]{0,1:T(8,128)(2,1)}) %all-gather.17.cloned.1.call-update) | async-done | bytes 2479120 | tf_op jit(solution)/shard_map/all_gather | solution.py:87
  374.9 49.4 %all-gather.15.cloned.1.call-done = bf16[1152,1076]{1,0:T(8,128)(2,1)} async-done(((bf16[144,1076]{1,0:T(8,128)(2,1)}), bf16[1152,1076]{1,0:T(8,128)(2,1)}) %all-gather.15.cloned.1.call-update) | async-done | bytes 2479120 | tf_op jit(solution)/shard_map/all_gather | solution.py:86
  424.3 20.5 %all-gather.13.cloned.1.call-done = bf16[736,1152]{1,0:T(8,128)(2,1)} async-done(((bf16[184,1152]{1,0:T(8,128)(2,1)}), bf16[736,1152]{1,0:T(8,128)(2,1)}) %all-gather.13.cloned.1.call-update) | async-done | bytes 1695760 | tf_op jit(solution)/shard_map/all_gather | solution.py:129
  473.1 15.4 %all-gather.21.cloned.1.call-done = bf16[736,1152]{1,0:T(8,128)(2,1)} async-done(((bf16[184,1152]{1,0:T(8,128)(2,1)}), bf16[736,1152]{1,0:T(8,128)(2,1)}) %all-gather.21.cloned.1.call-update) | async-done | bytes 1695760 | tf_op jit(solution)/shard_map/all_gather | solution.py:129
  520.2 10.4 reduce-scatter.51.cloned.1.call-done
  530.6 42.1 %reduce-scatter.55.cloned.1.call-done = f32[184,1152]{1,0:T(8,128)} async-done(((f32[736,1152]{1,0:T(8,128)}), f32[184,1152]{1,0:T(8,128)}) %reduce-scatter.55.cloned.1.call-update) | async-done | bytes 847888
  574.8 39.9 %reduce-scatter.45.cloned.1.call-done = f32[184,1152]{1,0:T(8,128)} async-done(((f32[736,1152]{1,0:T(8,128)}), f32[184,1152]{1,0:T(8,128)}) %reduce-scatter.45.cloned.1.call-update) | async-done | bytes 847888
  614.7 42.1 %reduce-scatter.49.cloned.1.call-done = f32[184,1152]{1,0:T(8,128)} async-done(((f32[736,1152]{1,0:T(8,128)}), f32[184,1152]{1,0:T(8,128)}) %reduce-scatter.49.cloned.1.call-update) | async-done | bytes 847888
  665.4 19.5 %all-gather.29.cloned.1.call-done = bf16[736,1152]{1,0:T(8,128)(2,1)} async-done(((bf16[184,1152]{1,0:T(8,128)(2,1)}), bf16[736,1152]{1,0:T(8,128)(2,1)}) %all-gather.29.cloned.1.call-update) | async-done | bytes 1695760 | tf_op jit(solution)/shard_map/all_gather | solution.py:213
  796.5 43.7 %all-reduce.14 = (f32[6,1152]{1,0:T(8,128)}, f32[2,1152]{1,0:T(2,128)S(1)}, f32[4304]{0:T(1024)S(1)}) all-reduce(f32[6,1152]{1,0:T(8,128)S(1)} %stack.38, f32[2,1152]{1,0:T(2,128)S(1)} %dynamic_update_slice.6, f32[4304]{0:T(1024)S(1)} %add_dynamic-update-slice_fusion), channel_id=1, replica_groups=mesh['fsdp'=8,'tp'=4] {'fsdp','tp'}, use_global_device_ids=true, to_apply=%region_42.43 | all-reduce | flops 13520 | bytes 108160 | tf_op jit(solution)/shard_map/psum | solution.py:344
  848.7 52.2 %reduce-scatter.39.cloned.1.call-done = f32[144,1076]{1,0:T(8,128)} async-done(((f32[1152,1076]{1,0:T(8,128)}), f32[144,1076]{1,0:T(8,128)}) %reduce-scatter.39.cloned.1.call-update) | async-done | bytes 619792 | tf_op jit(solution)/shard_map/reduce_scatter | solution.py:332
  901.0 108.4 %reduce-scatter.41.cloned.1.call-done = f32[1076,144]{0,1:T(8,128)} async-done(((f32[1076,1152]{0,1:T(8,128)}), f32[1076,144]{0,1:T(8,128)}) %reduce-scatter.41.cloned.1.call-update) | async-done | bytes 619792 | tf_op jit(solution)/shard_map/reduce_scatter | solution.py:333
  1009.4 69.9 %reduce-scatter.37.cloned.1.call-done = f32[288,144]{0,1:T(8,128)} async-done(((f32[288,1152]{0,1:T(8,128)}), f32[288,144]{0,1:T(8,128)}) %reduce-scatter.37.cloned.1.call-update) | async-done | bytes 165904 | tf_op jit(solution)/shard_map/reduce_scatter | solution.py:331
  1079.3 69.5 %reduce-scatter.35.cloned.1.call-done = f32[144,288]{1,0:T(8,128)} async-done(((f32[1152,288]{1,0:T(8,128)}), f32[144,288]{1,0:T(8,128)}) %reduce-scatter.35.cloned.1.call-update) | async-done | bytes 165904 | tf_op jit(solution)/shard_map/reduce_scatter | solution.py:330
  1148.7 69.0 %reduce-scatter.33.cloned.1.call-done = f32[144,288]{1,0:T(8,128)} async-done(((f32[1152,288]{1,0:T(8,128)}), f32[144,288]{1,0:T(8,128)}) %reduce-scatter.33.cloned.1.call-update) | async-done | bytes 165904 | tf_op jit(solution)/shard_map/reduce_scatter | solution.py:329
  1217.7 69.0 %reduce-scatter.31.cloned.1.call-done = f32[144,288]{1,0:T(8,128)} async-done(((f32[1152,288]{1,0:T(8,128)}), f32[144,288]{1,0:T(8,128)}) %reduce-scatter.31.cloned.1.call-update) | async-done | bytes 165904 | tf_op jit(solution)/shard_map/reduce_scatter | solution.py:328
  (425 shorter events, 254.7 us)
Async XLA Ops:
  7.2 185.3 %all-gather.19.cloned.1.call-start = ((), (), s32[]{:S(2)}) async-start(), calls=%async_computation.18 | async-start | bytes 2119680 | tf_op jit(solution)/shard_map/all_gather | solution.py:108
  59.2 151.7 %all-gather.11.cloned.1.call-start = ((), (), s32[]{:S(2)}) async-start(), calls=%async_computation.14 | async-start | bytes 2119680 | tf_op jit(solution)/shard_map/all_gather | solution.py:108
  60.0 187.0 %reduce-scatter.47.cloned.1.call-start = ((), (), s32[]{:S(2)}) async-start(), calls=%async_computation.32 | async-start | bytes 4239360
  209.9 79.2 %reduce-scatter.43.cloned.1.call-start = ((), (), s32[]{:S(2)}) async-start(), calls=%async_computation.30 | async-start | bytes 4239360
  227.8 83.6 %all-gather.23.cloned.1.call-start = ((), (), s32[]{:S(2)}) async-start(), calls=%async_computation.20 | async-start | bytes 2119680 | tf_op jit(solution)/shard_map/all_gather | solution.py:194
  230.5 138.0 %all-gather.17.cloned.1.call-start = ((), (), s32[]{:S(2)}) async-start(), calls=%async_computation.17 | async-start | bytes 2985984 | tf_op jit(solution)/shard_map/all_gather | solution.py:87
  231.1 193.2 %all-gather.15.cloned.1.call-start = ((), (), s32[]{:S(2)}) async-start(), calls=%async_computation.16 | async-start | bytes 2985984 | tf_op jit(solution)/shard_map/all_gather | solution.py:86
  231.8 213.0 %all-gather.13.cloned.1.call-start = ((), (), s32[]{:S(2)}) async-start(), calls=%async_computation.15 | async-start | bytes 2119680 | tf_op jit(solution)/shard_map/all_gather | solution.py:129
  292.6 174.2 %all-gather.27.cloned.1.call-start = ((), (), s32[]{:S(2)}) async-start(), calls=%async_computation.22 | async-start | bytes 2119680 | tf_op jit(solution)/shard_map/all_gather | solution.py:194
  293.3 195.2 %all-gather.21.cloned.1.call-start = ((), (), s32[]{:S(2)}) async-start(), calls=%async_computation.19 | async-start | bytes 2119680 | tf_op jit(solution)/shard_map/all_gather | solution.py:129
  293.9 236.7 %reduce-scatter.51.cloned.1.call-start = ((), (), s32[]{:S(2)}) async-start(), calls=%async_computation.34 | async-start | bytes 4239360
  460.8 111.9 %reduce-scatter.55.cloned.1.call-start = ((), (), s32[]{:S(2)}) async-start(), calls=%async_computation.36 | async-start | bytes 4239360
  504.3 110.3 %reduce-scatter.45.cloned.1.call-start = ((), (), s32[]{:S(2)}) async-start(), calls=%async_computation.31 | async-start | bytes 4239360
  512.4 144.3 %reduce-scatter.49.cloned.1.call-start = ((), (), s32[]{:S(2)}) async-start(), calls=%async_computation.33 | async-start | bytes 4239360
  520.1 164.7 %all-gather.29.cloned.1.call-start = ((), (), s32[]{:S(2)}) async-start(), calls=%async_computation.23 | async-start | bytes 2119680 | tf_op jit(solution)/shard_map/all_gather | solution.py:213
  664.4 45.6 %all-gather.25.cloned.1.call-start = ((), (), s32[]{:S(2)}) async-start(), calls=%async_computation.21 | async-start | bytes 2119680 | tf_op jit(solution)/shard_map/all_gather | solution.py:213
  665.0 117.2 %reduce-scatter.57.cloned.1.call-start = ((), (), s32[]{:S(2)}) async-start(), calls=%async_computation.37 | async-start | bytes 4239360
  709.8 81.7 %reduce-scatter.53.cloned.1.call-start = ((), (), s32[]{:S(2)}) async-start(), calls=%async_computation.35 | async-start | bytes 4239360
  734.7 166.2 %reduce-scatter.39.cloned.1.call-start = ((), (), s32[]{:S(2)}) async-start(), calls=%async_computation.28 | async-start | bytes 5971968 | tf_op jit(solution)/shard_map/reduce_scatter | solution.py:332
  745.5 263.9 %reduce-scatter.41.cloned.1.call-start = ((), (), s32[]{:S(2)}) async-start(), calls=%async_computation.29 | async-start | bytes 5971968 | tf_op jit(solution)/shard_map/reduce_scatter | solution.py:333
  756.8 322.4 %reduce-scatter.37.cloned.1.call-start = ((), (), s32[]{:S(2)}) async-start(), calls=%async_computation.27 | async-start | bytes 1990656 | tf_op jit(solution)/shard_map/reduce_scatter | solution.py:331
  763.1 385.7 %reduce-scatter.35.cloned.1.call-start = ((), (), s32[]{:S(2)}) async-start(), calls=%async_computation.26 | async-start | bytes 1990656 | tf_op jit(solution)/shard_map/reduce_scatter | solution.py:330
  768.3 449.4 %reduce-scatter.33.cloned.1.call-start = ((), (), s32[]{:S(2)}) async-start(), calls=%async_computation.25 | async-start | bytes 1990656 | tf_op jit(solution)/shard_map/reduce_scatter | solution.py:329
  773.5 513.2 %reduce-scatter.31.cloned.1.call-start = ((), (), s32[]{:S(2)}) async-start(), calls=%async_computation.24 | async-start | bytes 1990656 | tf_op jit(solution)/shard_map/reduce_scatter | solution.py:328
  (114 other events, 1805.3 us)
Sparse Core Ops, SparseCore 0:
  59.3 17.5 all-gather.18
  79.0 20.3 all-gather.10
  210.0 36.9 reduce-scatter.46
  249.5 39.4 reduce-scatter.42
  291.0 20.3 all-gather.22
  313.4 55.0 all-gather.16
  370.6 53.5 all-gather.14
  425.8 18.9 all-gather.12
  446.4 20.3 all-gather.26
  468.1 20.3 all-gather.20
  491.1 39.4 reduce-scatter.50
  533.1 39.4 reduce-scatter.54
  575.2 39.4 reduce-scatter.44
  617.2 39.4 reduce-scatter.48
  664.5 20.3 all-gather.28
  686.3 20.3 all-gather.24
  709.9 39.4 reduce-scatter.56
  752.0 39.4 reduce-scatter.52
  795.6 105.2 reduce-scatter.38
  905.4 103.9 reduce-scatter.40
  1013.4 65.7 reduce-scatter.36
  1083.7 64.9 reduce-scatter.34
  1152.8 64.8 reduce-scatter.32
  1222.0 64.6 reduce-scatter.30
where the time goes:
time: 1300 us; the launch traced here: 1290 us
  waiting for transfers between devices  827 us (64%)
  blocking collectives  214 us (16%)
  matrix products  156 us (12%)
  other arithmetic  50 us (4%)
  local copies, waits for them, and re-layouts  26.7 us (2%)
  between operations  17.3 us (1%)
    unnamed x32, waiting for transfers between devices  205 us
    reduce_scatter x1, waiting for transfers between devices, local(): lax.psum_scatter(grad_w_down, 'fsdp', scatter_dimension=1, tiled=True)  108 us
    reduce_scatter x1, waiting for transfers between devices, local(): lax.psum_scatter(grad_w_out, 'fsdp', scatter_dimension=1, tiled=True)  69.9 us
    reduce_scatter x1, waiting for transfers between devices, local(): lax.psum_scatter(grad_wv, 'fsdp', scatter_dimension=0, tiled=True)  69.5 us
    reduce_scatter x1, waiting for transfers between devices, local(): lax.psum_scatter(grad_wq, 'fsdp', scatter_dimension=0, tiled=True)  69 us
    reduce_scatter x1, waiting for transfers between devices, local(): lax.psum_scatter(grad_wk, 'fsdp', scatter_dimension=0, tiled=True)  69 us
    all_gather x1, waiting for transfers between devices, fetch_weights(): lax.all_gather(down_weight, 'fsdp', axis=1, tiled=True)  57.1 us
    reduce_scatter x1, waiting for transfers between devices, local(): lax.psum_scatter(grad_w_up, 'fsdp', scatter_dimension=0, tiled=True)  52.2 us
  transfers between devices with their start and end apart: 24, of which 20 were waited for; matrix products, arithmetic and copies ran while one was open for 15% of the time, Pallas kernels for 0%

commit v1 on v0

--- a/solution.py
+++ b/solution.py
@@ -6,6 +6,29 @@
 HD = 72
 epsilon = 1e-06
 negative_big = -1e30
+
+
+def laid_out(blocks, dim):
+    blocks = jnp.moveaxis(blocks, 0, dim)
+    shape = blocks.shape
+    return blocks.reshape(*shape[:dim], shape[dim] * shape[dim + 1], *shape[dim + 2 :])
+
+
+def collected_by_bits(x, axis):
+    size, index = (lax.axis_size(axis), lax.axis_index(axis))
+    blocks, stride = (x[None], 1)
+    while stride < size:
+        partner_block = lax.ppermute(blocks, axis, [(i, i ^ stride) for i in range(size)])
+        low = index & stride == 0
+        blocks = jnp.concatenate(
+            [jnp.where(low, blocks, partner_block), jnp.where(low, partner_block, blocks)]
+        )
+        stride *= 2
+    return blocks
+
+
+def gather_by_bits(x, axis, dim):
+    return laid_out(collected_by_bits(x, axis), dim)
 
 
 def layer_norm(row_block, gain_vec, shift_vec):
@@ -74,7 +97,7 @@
         attn_full = (
             lax.all_gather(ln1_gain, "fsdp", axis=0, tiled=True),
             lax.all_gather(ln1_bias, "fsdp", axis=0, tiled=True),
-            lax.all_gather(q_weight, "fsdp", axis=0, tiled=True),
+            gather_by_bits(q_weight, "fsdp", 0),
             lax.all_gather(k_weight, "fsdp", axis=0, tiled=True),
             lax.all_gather(v_weight, "fsdp", axis=0, tiled=True),
             lax.all_gather(out_weight, "fsdp", axis=1, tiled=True),

time: 1300 us -> 1270 us (0.977)
  blocking collectives: 214 us -> 185 us
    all_gather x1 -> x0, blocking collectives: 32.5 us -> none  [fetch_weights(): lax.all_gather(q_weight, 'fsdp', axis=0, tiled=True)]
  transfers between devices with their start and end apart: 24 -> 27, of which waited for: 20 -> 20; matrix products, arithmetic and copies ran while one was open for 15% -> 16% of each run, Pallas kernels for 0% -> 0%
where the time goes in v1:
time: 1270 us
  waiting for transfers between devices  833 us (66%)
  blocking collectives  185 us (15%)
  matrix products  154 us (12%)
  other arithmetic  50.7 us (4%)
  local copies, waits for them, and re-layouts  25.2 us (2%)
  between operations  17.2 us (1%)
    unnamed x32, waiting for transfers between devices  209 us
    reduce_scatter x1, waiting for transfers between devices, local(): lax.psum_scatter(grad_w_down, 'fsdp', scatter_dimension=1, tiled=True)  108 us
    reduce_scatter x1, waiting for transfers between devices, local(): lax.psum_scatter(grad_w_out, 'fsdp', scatter_dimension=1, tiled=True)  69.8 us
    reduce_scatter x1, waiting for transfers between devices, local(): lax.psum_scatter(grad_wv, 'fsdp', scatter_dimension=0, tiled=True)  69.6 us
    reduce_scatter x1, waiting for transfers between devices, local(): lax.psum_scatter(grad_wq, 'fsdp', scatter_dimension=0, tiled=True)  69.5 us
    reduce_scatter x1, waiting for transfers between devices, local(): lax.psum_scatter(grad_wk, 'fsdp', scatter_dimension=0, tiled=True)  68.8 us
    all_gather x1, waiting for transfers between devices, fetch_weights(): lax.all_gather(down_weight, 'fsdp', axis=1, tiled=True)  57.1 us
    reduce_scatter x1, waiting for transfers between devices, local(): lax.psum_scatter(grad_w_up, 'fsdp', scatter_dimension=0, tiled=True)  52.9 us
  transfers between devices with their start and end apart: 27, of which 20 were waited for; matrix products, arithmetic and copies ran while one was open for 16% of the time, Pallas kernels for 0%

profile of v1, /device:TPU:0, one launch (start us, length us, event | category | flops | bytes accessed | tf_op | source)
XLA Modules:
  0.0 1268.0 jit_solution(742294355445181545)
XLA Ops:
  14.3 39.4 %all-reduce.15 = (bf16[1152]{0:T(1024)(128)(2,1)S(1)}, bf16[1152]{0:T(1024)(128)(2,1)S(1)}, bf16[1152]{0:T(1024)(128)(2,1)}, bf16[1152]{0:T(1024)(128)(2,1)}, bf...) all-reduce(bf16[1152]{0:T(1024)(128)(2,1)S(1)} %dynamic-update-slice.1, ...), channel_id=1, replica_groups=mesh['fsdp'=8,'tp'=4] {'fsdp'}, use_global_device_ids=true, to_apply=%add.1 | all-reduce | flops 6912 | bytes 27648
  60.6 32.9 %all_gather.42 = bf16[1152,288]{1,0:T(8,128)(2,1)S(1)} all-gather(bf16[144,288]{1,0:T(8,128)(2,1)S(1)} %copy-done.56), channel_id=1, replica_groups=mesh['fsdp'=8,'tp'=4] {'fsdp'}, dimensions={0}, use_global_device_ids=true | all-gather | bytes 746496 | tf_op jit(solution)/shard_map/all_gather | solution.py:101
  93.7 32.7 %all_gather.41 = bf16[1152,288]{1,0:T(8,128)(2,1)S(1)} all-gather(bf16[144,288]{1,0:T(8,128)(2,1)S(1)} %copy-done.57), channel_id=1, replica_groups=mesh['fsdp'=8,'tp'=4] {'fsdp'}, dimensions={0}, use_global_device_ids=true | all-gather | bytes 746496 | tf_op jit(solution)/shard_map/all_gather | solution.py:102
  128.7 35.9 %all_gather.43 = bf16[288,1152]{0,1:T(8,128)(2,1)S(1)} all-gather(bf16[288,144]{0,1:T(8,128)(2,1)S(1)} %copy-done.58), channel_id=1, replica_groups=mesh['fsdp'=8,'tp'=4] {'fsdp'}, dimensions={1}, use_global_device_ids=true | all-gather | bytes 746496 | tf_op jit(solution)/shard_map/all_gather | solution.py:103
  206.5 15.7 %reduce-scatter.47.cloned.1.call-done = f32[184,1152]{1,0:T(8,128)} async-done(((f32[736,1152]{1,0:T(8,128)}), f32[184,1152]{1,0:T(8,128)}) %reduce-scatter.47.cloned.1.call-update) | async-done | bytes 847888
  222.2 42.1 %reduce-scatter.43.cloned.1.call-done = f32[184,1152]{1,0:T(8,128)} async-done(((f32[736,1152]{1,0:T(8,128)}), f32[184,1152]{1,0:T(8,128)}) %reduce-scatter.43.cloned.1.call-update) | async-done | bytes 847888
  269.7 16.9 %all-gather.23.cloned.1.call-done = bf16[736,1152]{1,0:T(8,128)(2,1)} async-done(((bf16[184,1152]{1,0:T(8,128)(2,1)}), bf16[736,1152]{1,0:T(8,128)(2,1)}) %all-gather.23.cloned.1.call-update) | async-done | bytes 1695760 | tf_op jit(solution)/shard_map/all_gather | solution.py:217
  286.6 57.1 %all-gather.17.cloned.1.call-done = bf16[1076,1152]{0,1:T(8,128)(2,1)} async-done(((bf16[1076,144]{0,1:T(8,128)(2,1)}), bf16[1076,1152]{0,1:T(8,128)(2,1)}) %all-gather.17.cloned.1.call-update) | async-done | bytes 2479120 | tf_op jit(solution)/shard_map/all_gather | solution.py:110
  350.2 49.4 %all-gather.15.cloned.1.call-done = bf16[1152,1076]{1,0:T(8,128)(2,1)} async-done(((bf16[144,1076]{1,0:T(8,128)(2,1)}), bf16[1152,1076]{1,0:T(8,128)(2,1)}) %all-gather.15.cloned.1.call-update) | async-done | bytes 2479120 | tf_op jit(solution)/shard_map/all_gather | solution.py:109
  399.5 20.5 %all-gather.13.cloned.1.call-done = bf16[736,1152]{1,0:T(8,128)(2,1)} async-done(((bf16[184,1152]{1,0:T(8,128)(2,1)}), bf16[736,1152]{1,0:T(8,128)(2,1)}) %all-gather.13.cloned.1.call-update) | async-done | bytes 1695760 | tf_op jit(solution)/shard_map/all_gather | solution.py:152
  448.4 15.4 %all-gather.21.cloned.1.call-done = bf16[736,1152]{1,0:T(8,128)(2,1)} async-done(((bf16[184,1152]{1,0:T(8,128)(2,1)}), bf16[736,1152]{1,0:T(8,128)(2,1)}) %all-gather.21.cloned.1.call-update) | async-done | bytes 1695760 | tf_op jit(solution)/shard_map/all_gather | solution.py:152
  495.5 10.4 reduce-scatter.51.cloned.1.call-done
  505.8 42.1 %reduce-scatter.55.cloned.1.call-done = f32[184,1152]{1,0:T(8,128)} async-done(((f32[736,1152]{1,0:T(8,128)}), f32[184,1152]{1,0:T(8,128)}) %reduce-scatter.55.cloned.1.call-update) | async-done | bytes 847888
  550.0 39.9 %reduce-scatter.45.cloned.1.call-done = f32[184,1152]{1,0:T(8,128)} async-done(((f32[736,1152]{1,0:T(8,128)}), f32[184,1152]{1,0:T(8,128)}) %reduce-scatter.45.cloned.1.call-update) | async-done | bytes 847888
  589.9 42.1 %reduce-scatter.49.cloned.1.call-done = f32[184,1152]{1,0:T(8,128)} async-done(((f32[736,1152]{1,0:T(8,128)}), f32[184,1152]{1,0:T(8,128)}) %reduce-scatter.49.cloned.1.call-update) | async-done | bytes 847888
  640.0 19.5 %all-gather.29.cloned.1.call-done = bf16[736,1152]{1,0:T(8,128)(2,1)} async-done(((bf16[184,1152]{1,0:T(8,128)(2,1)}), bf16[736,1152]{1,0:T(8,128)(2,1)}) %all-gather.29.cloned.1.call-update) | async-done | bytes 1695760 | tf_op jit(solution)/shard_map/all_gather | solution.py:236
  752.1 13.2 %reduce-scatter.53.cloned.1.call-done = f32[184,1152]{1,0:T(8,128)} async-done(((f32[736,1152]{1,0:T(8,128)}), f32[184,1152]{1,0:T(8,128)}) %reduce-scatter.53.cloned.1.call-update) | async-done | bytes 847888
  770.3 43.7 %all-reduce.14 = (f32[6,1152]{1,0:T(8,128)}, f32[2,1152]{1,0:T(2,128)S(1)}, f32[4304]{0:T(1024)S(1)}) all-reduce(f32[6,1152]{1,0:T(8,128)S(1)} %stack.38, f32[2,1152]{1,0:T(2,128)S(1)} %dynamic_update_slice.6, f32[4304]{0:T(1024)S(1)} %add_dynamic-update-slice_fusion), channel_id=1, replica_groups=mesh['fsdp'=8,'tp'=4] {'fsdp','tp'}, use_global_device_ids=true, to_apply=%region_42.43 | all-reduce | flops 13520 | bytes 108160 | tf_op jit(solution)/shard_map/psum | solution.py:367
  821.8 52.9 %reduce-scatter.39.cloned.1.call-done = f32[144,1076]{1,0:T(8,128)} async-done(((f32[1152,1076]{1,0:T(8,128)}), f32[144,1076]{1,0:T(8,128)}) %reduce-scatter.39.cloned.1.call-update) | async-done | bytes 619792 | tf_op jit(solution)/shard_map/reduce_scatter | solution.py:355
  874.6 108.4 %reduce-scatter.41.cloned.1.call-done = f32[1076,144]{0,1:T(8,128)} async-done(((f32[1076,1152]{0,1:T(8,128)}), f32[1076,144]{0,1:T(8,128)}) %reduce-scatter.41.cloned.1.call-update) | async-done | bytes 619792 | tf_op jit(solution)/shard_map/reduce_scatter | solution.py:356
  983.0 69.8 %reduce-scatter.37.cloned.1.call-done = f32[288,144]{0,1:T(8,128)} async-done(((f32[288,1152]{0,1:T(8,128)}), f32[288,144]{0,1:T(8,128)}) %reduce-scatter.37.cloned.1.call-update) | async-done | bytes 165904 | tf_op jit(solution)/shard_map/reduce_scatter | solution.py:354
  1052.8 69.6 %reduce-scatter.35.cloned.1.call-done = f32[144,288]{1,0:T(8,128)} async-done(((f32[1152,288]{1,0:T(8,128)}), f32[144,288]{1,0:T(8,128)}) %reduce-scatter.35.cloned.1.call-update) | async-done | bytes 165904 | tf_op jit(solution)/shard_map/reduce_scatter | solution.py:353
  1122.4 68.8 %reduce-scatter.33.cloned.1.call-done = f32[144,288]{1,0:T(8,128)} async-done(((f32[1152,288]{1,0:T(8,128)}), f32[144,288]{1,0:T(8,128)}) %reduce-scatter.33.cloned.1.call-update) | async-done | bytes 165904 | tf_op jit(solution)/shard_map/reduce_scatter | solution.py:352
  1191.3 69.5 %reduce-scatter.31.cloned.1.call-done = f32[144,288]{1,0:T(8,128)} async-done(((f32[1152,288]{1,0:T(8,128)}), f32[144,288]{1,0:T(8,128)}) %reduce-scatter.31.cloned.1.call-update) | async-done | bytes 165904 | tf_op jit(solution)/shard_map/reduce_scatter | solution.py:351
  (412 shorter events, 242.9 us)
Async XLA Ops:
  7.2 160.0 %all-gather.19.cloned.1.call-start = ((), (), s32[]{:S(2)}) async-start(), calls=%async_computation.18 | async-start | bytes 2119680 | tf_op jit(solution)/shard_map/all_gather | solution.py:131
  59.7 124.9 %all-gather.11.cloned.1.call-start = ((), (), s32[]{:S(2)}) async-start(), calls=%async_computation.14 | async-start | bytes 2119680 | tf_op jit(solution)/shard_map/all_gather | solution.py:131
  60.5 161.7 %reduce-scatter.47.cloned.1.call-start = ((), (), s32[]{:S(2)}) async-start(), calls=%async_computation.32 | async-start | bytes 4239360
  183.6 80.7 %reduce-scatter.43.cloned.1.call-start = ((), (), s32[]{:S(2)}) async-start(), calls=%async_computation.30 | async-start | bytes 4239360
  202.4 84.2 %all-gather.23.cloned.1.call-start = ((), (), s32[]{:S(2)}) async-start(), calls=%async_computation.20 | async-start | bytes 2119680 | tf_op jit(solution)/shard_map/all_gather | solution.py:217
  205.0 138.7 %all-gather.17.cloned.1.call-start = ((), (), s32[]{:S(2)}) async-start(), calls=%async_computation.17 | async-start | bytes 2985984 | tf_op jit(solution)/shard_map/all_gather | solution.py:110
  205.6 193.9 %all-gather.15.cloned.1.call-start = ((), (), s32[]{:S(2)}) async-start(), calls=%async_computation.16 | async-start | bytes 2985984 | tf_op jit(solution)/shard_map/all_gather | solution.py:109
  206.4 213.7 %all-gather.13.cloned.1.call-start = ((), (), s32[]{:S(2)}) async-start(), calls=%async_computation.15 | async-start | bytes 2119680 | tf_op jit(solution)/shard_map/all_gather | solution.py:152
  267.9 174.1 %all-gather.27.cloned.1.call-start = ((), (), s32[]{:S(2)}) async-start(), calls=%async_computation.22 | async-start | bytes 2119680 | tf_op jit(solution)/shard_map/all_gather | solution.py:217
  268.6 195.2 %all-gather.21.cloned.1.call-start = ((), (), s32[]{:S(2)}) async-start(), calls=%async_computation.19 | async-start | bytes 2119680 | tf_op jit(solution)/shard_map/all_gather | solution.py:152
  269.2 236.7 %reduce-scatter.51.cloned.1.call-start = ((), (), s32[]{:S(2)}) async-start(), calls=%async_computation.34 | async-start | bytes 4239360
  436.1 111.8 %reduce-scatter.55.cloned.1.call-start = ((), (), s32[]{:S(2)}) async-start(), calls=%async_computation.36 | async-start | bytes 4239360
  479.6 110.3 %reduce-scatter.45.cloned.1.call-start = ((), (), s32[]{:S(2)}) async-start(), calls=%async_computation.31 | async-start | bytes 4239360
  487.7 144.3 %reduce-scatter.49.cloned.1.call-start = ((), (), s32[]{:S(2)}) async-start(), calls=%async_computation.33 | async-start | bytes 4239360
  495.4 164.1 %all-gather.29.cloned.1.call-start = ((), (), s32[]{:S(2)}) async-start(), calls=%async_computation.23 | async-start | bytes 2119680 | tf_op jit(solution)/shard_map/all_gather | solution.py:236
  639.0 42.5 %all-gather.25.cloned.1.call-start = ((), (), s32[]{:S(2)}) async-start(), calls=%async_computation.21 | async-start | bytes 2119680 | tf_op jit(solution)/shard_map/all_gather | solution.py:236
  639.6 112.5 %reduce-scatter.57.cloned.1.call-start = ((), (), s32[]{:S(2)}) async-start(), calls=%async_computation.37 | async-start | bytes 4239360
  681.2 84.0 %reduce-scatter.53.cloned.1.call-start = ((), (), s32[]{:S(2)}) async-start(), calls=%async_computation.35 | async-start | bytes 4239360
  705.1 169.5 %reduce-scatter.39.cloned.1.call-start = ((), (), s32[]{:S(2)}) async-start(), calls=%async_computation.28 | async-start | bytes 5971968 | tf_op jit(solution)/shard_map/reduce_scatter | solution.py:355
  715.8 267.2 %reduce-scatter.41.cloned.1.call-start = ((), (), s32[]{:S(2)}) async-start(), calls=%async_computation.29 | async-start | bytes 5971968 | tf_op jit(solution)/shard_map/reduce_scatter | solution.py:356
  727.2 325.6 %reduce-scatter.37.cloned.1.call-start = ((), (), s32[]{:S(2)}) async-start(), calls=%async_computation.27 | async-start | bytes 1990656 | tf_op jit(solution)/shard_map/reduce_scatter | solution.py:354
  733.5 388.9 %reduce-scatter.35.cloned.1.call-start = ((), (), s32[]{:S(2)}) async-start(), calls=%async_computation.26 | async-start | bytes 1990656 | tf_op jit(solution)/shard_map/reduce_scatter | solution.py:353
  739.1 452.2 %reduce-scatter.33.cloned.1.call-start = ((), (), s32[]{:S(2)}) async-start(), calls=%async_computation.25 | async-start | bytes 1990656 | tf_op jit(solution)/shard_map/reduce_scatter | solution.py:352
  744.2 516.5 %reduce-scatter.31.cloned.1.call-start = ((), (), s32[]{:S(2)}) async-start(), calls=%async_computation.24 | async-start | bytes 1990656 | tf_op jit(solution)/shard_map/reduce_scatter | solution.py:351
  (105 other events, 1723.4 us)
Sparse Core Ops, SparseCore 0:
  59.9 17.5 all-gather.18
  79.6 20.3 all-gather.10
  183.7 38.4 reduce-scatter.46
  224.8 39.4 reduce-scatter.42
  266.3 20.3 all-gather.22
  288.7 55.0 all-gather.16
  345.9 53.5 all-gather.14
  401.1 18.9 all-gather.12
  421.6 20.3 all-gather.26
  443.4 20.3 all-gather.20
  466.3 39.4 reduce-scatter.50
  508.4 39.4 reduce-scatter.54
  550.4 39.4 reduce-scatter.44
  592.5 39.4 reduce-scatter.48
  639.1 20.3 all-gather.28
  660.9 20.3 all-gather.24
  683.7 39.4 reduce-scatter.56
  725.8 39.4 reduce-scatter.52
  769.4 105.1 reduce-scatter.38
  879.1 103.9 reduce-scatter.40
  987.1 65.7 reduce-scatter.36
  1057.2 65.1 reduce-scatter.34
  1126.5 64.7 reduce-scatter.32
  1195.5 65.1 reduce-scatter.30
